TPU v7x, 32 devices: a whole 2x2x4 slice. The times are simulated.
32 devices in a mesh: gz: 8 (over z, core), pair: 4 (over y, x).
Axes of the slice: x: 2, y: 2, z: 4, core: 2. Of those that a mesh axis runs over, the one named last changes fastest.
Arguments:
- orbitals: bfloat16 [8, 64, 256, 256], P(None, 'gz'), may hold values from -6 to 6
- pair_index: int32 [4, 2], P('pair'), may hold values from 0 to 7
- pair_weight: float32 [4], P('pair'), may hold values from 0.5 to 2
Outputs:
- potential: float32 [4, 64, 256, 256], P('pair', 'gz')
- residual_norm: float32 [4], P('pair')
- energy: float32 [1], replicated
Inputs may be any that keep to these rules, and one draw needn't show every extreme that they name: `pair_index`: A pair may name one orbital twice.
All inputs are finite; a program needn't handle non-finite values.
Results may differ from a plain program's by a relative error of at most 0.0003.
Values sent between devices are 32-bit elements; how exact they have to be, the bound alone decides.
No kernel may reach another device: no remote copies, remote signals or barrier semaphores. Data moves between devices by JAX's collectives and lax.ppermute only.
A program may use at most 320 MiB of HBM per device.

v0:
```python
import jax
import jax.numpy as jnp
from jax import lax
from jax.sharding import PartitionSpec as P

LEVELS = 4
NU = 2
COARSE = 8
relax = 2.0 / 3.0


def with_halo(block, sides, width):
    for axis, dim in sides:
        count = lax.axis_size(axis)
        forward = [(i, i + 1) for i in range(count - 1)]
        backward = [(target, source) for source, target in forward]
        low = lax.ppermute(
            lax.slice_in_dim(block, block.shape[dim] - width, None, axis=dim), axis, forward
        )
        high = lax.ppermute(lax.slice_in_dim(block, 0, width, axis=dim), axis, backward)
        block = jnp.concatenate([low, block, high], axis=dim)
    return block


def apply_op(field, level):
    extended = with_halo(field, (("gz", 1),), 1)
    padded = jnp.pad(field, ((0, 0), (0, 0), (1, 1), (1, 1)))
    beside = extended[:, 2:] + extended[:, :-2]
    beside = beside + padded[:, :, 2:, 1:-1] + padded[:, :, :-2, 1:-1]
    beside = beside + padded[:, :, 1:-1, 2:] + padded[:, :, 1:-1, :-2]
    return (6.0 * field - beside) * 0.25**level


def local_op(field, level):
    padded = jnp.pad(field, ((0, 0), (1, 1), (1, 1), (1, 1)))
    beside = padded[:, 2:, 1:-1, 1:-1] + padded[:, :-2, 1:-1, 1:-1]
    beside = beside + padded[:, 1:-1, 2:, 1:-1] + padded[:, 1:-1, :-2, 1:-1]
    beside = beside + padded[:, 1:-1, 1:-1, 2:] + padded[:, 1:-1, 1:-1, :-2]
    return (6.0 * field - beside) * 0.25**level


def sweep(field, source, level):
    return field + (source - apply_op(field, level)) * (relax * 4.0**level / 6.0)


def restrict(field):
    pairs, zsize, ysize, xsize = field.shape
    return field.reshape(pairs, zsize // 2, 2, ysize // 2, 2, xsize // 2, 2).mean(axis=(2, 4, 6))


def prolong(field):
    return jnp.repeat(jnp.repeat(jnp.repeat(field, 2, axis=1), 2, axis=2), 2, axis=3)


def coarsest(source, level):
    gathered = lax.all_gather(source, "gz", axis=1, tiled=True)
    field = jnp.zeros_like(gathered)
    for _ in range(COARSE):
        field = field + (gathered - local_op(field, level)) * (relax * 4.0**level / 6.0)
    planes = source.shape[1]
    return lax.dynamic_slice_in_dim(field, lax.axis_index("gz") * planes, planes, 1)


def vcycle(field, source, level):
    if level == LEVELS - 1:
        return coarsest(source, level)
    for _ in range(NU):
        field = sweep(field, source, level)
    remain = source - apply_op(field, level)
    coarse_source = restrict(remain)
    correction = vcycle(jnp.zeros_like(coarse_source), coarse_source, level + 1)
    field = field + prolong(correction)
    for _ in range(NU):
        field = sweep(field, source, level)
    return field


def solve(density):
    field = jnp.zeros_like(density)
    field = vcycle(field, density, 0)
    return field


def per_device(orbitals, pair_index, pair_weight):
    left_orbital = jnp.take(orbitals, pair_index[:, 0], axis=0).astype(jnp.float32)
    right_orbital = jnp.take(orbitals, pair_index[:, 1], axis=0).astype(jnp.float32)
    density = left_orbital * right_orbital
    potential = solve(density)
    final = density - apply_op(potential, 0)
    totals = lax.psum(
        (jnp.sum(final * final, axis=(1, 2, 3)), jnp.sum(density * potential, axis=(1, 2, 3))), "gz"
    )
    cell_count = density.shape[1] * lax.axis_size("gz") * density.shape[2] * density.shape[3]
    residual_norm = jnp.sqrt(totals[0] / cell_count)
    partial_energy = -0.5 * jnp.sum(pair_weight * totals[1]) / cell_count
    energy = lax.psum(partial_energy, "pair").reshape(1)
    return (potential, residual_norm, energy)


def solution(mesh):
    return jax.shard_map(
        per_device,
        mesh=mesh,
        in_specs=(P(None, "gz", None, None), P("pair", None), P("pair")),
        out_specs=(P("pair", "gz", None, None), P("pair"), P()),
        check_vma=False,
    )
```

profile of v0, /device:TPU:0, one launch (start us, length us, event | category | flops | bytes accessed | tf_op | source)
XLA Modules:
  0.0 407.4 jit_solution(4606733979402125156)
XLA Ops:
  2.8 3.7 collective-permute-start.1
  6.5 1.3 fusion.235
  11.7 1.7 constant_dynamic-slice_fusion.1
  15.6 2.7 broadcast_multiply_fusion
  18.7 1.3 collective-permute-start.2
  20.0 4.5 %collective-permute-start.3 = (f32[1,1,256,256]{2,1,3,0:T(1,128)S(1)}, f32[1,1,256,256]{2,1,3,0:T(1,128)S(1)}, u32[]{:S(2)}, u32[]{:S(2)}) collective-permute-start(f32[1,1,256,256]{2,1,3,0:T(1,128)S(1)} %get-tuple-element.46), channel_id=1, source_target_pairs={{0,4},{4,8},{8,12},{12,16},{16,20},{20,24},{24,28},{1,5},{5,9},{9,... | collective-permute-start | bytes 786440 | tf_op jit(solution)/shard_map/ppermute | solution.py:17
  25.7 2.3 fusion.14
  28.3 1.3 collective-permute-start.4
  29.6 6.4 %collective-permute-start.5 = (f32[1,1,256,256]{2,1,3,0:T(1,128)S(1)}, f32[1,1,256,256]{2,1,3,0:T(1,128)S(1)}, u32[]{:S(2)}, u32[]{:S(2)}) collective-permute-start(f32[1,1,256,256]{2,1,3,0:T(1,128)S(1)} %get-tuple-element.44), channel_id=1, source_target_pairs={{0,4},{4,8},{8,12},{12,16},{16,20},{20,24},{24,28},{1,5},{5,9},{9,... | collective-permute-start | bytes 786440 | tf_op jit(solution)/shard_map/ppermute | solution.py:17
  36.1 1.3 collective-permute-start.6
  37.4 5.0 %collective-permute-start.7 = (f32[1,1,128,128]{3,2,1,0:T(8,128)S(1)}, f32[1,1,128,128]{3,2,1,0:T(8,128)S(1)}, u32[]{:S(2)}, u32[]{:S(2)}) collective-permute-start(f32[1,1,128,128]{3,2,1,0:T(8,128)S(1)} %broadcast.203), channel_id=1, source_target_pairs={{0,4},{4,8},{8,12},{12,16},{16,20},{20,24},{24,28},{1,5},{5,9},{9,... | collective-permute-start | bytes 196616 | tf_op jit(solution)/shard_map/ppermute | solution.py:17
  42.4 3.1 fusion.20
  45.5 3.0 copy.35
  48.4 136.2 %reshape.102 = f32[4,2,128,2,128,2]{5,4,3,2,1,0:T(8,128)} reshape(f32[1,8,256,256]{3,2,1,0:T(8,128)} %copy.35) | data formatting | bytes 4194304 | tf_op jit(solution)/shard_map/reshape | solution.py:48
  184.6 40.6 %reduce_sum.60 = f32[4,128,128]{2,1,0:T(8,128)S(1)} reduce(f32[4,2,128,2,128,2]{5,4,3,2,1,0:T(8,128)} %reshape.102, f32[]{:T(128)} %constant.30.clone.1), dimensions={1,3,5}, to_apply=%region_0.0 | reduce | flops 458752 | bytes 2359300 | tf_op jit(solution)/shard_map/reduce_sum | solution.py:48
  225.5 1.3 collective-permute-start.8
  226.8 4.3 %collective-permute-start.9 = (f32[1,1,128,128]{3,2,1,0:T(8,128)S(1)}, f32[1,1,128,128]{3,2,1,0:T(8,128)S(1)}, u32[]{:S(2)}, u32[]{:S(2)}) collective-permute-start(f32[1,1,128,128]{3,2,1,0:T(8,128)S(1)} %get-tuple-element.54), channel_id=1, source_target_pairs={{0,4},{4,8},{8,12},{12,16},{16,20},{20,24},{24,28},{1,5},{5,9},{9,... | collective-permute-start | bytes 196616 | tf_op jit(solution)/shard_map/ppermute | solution.py:17
  232.2 1.3 collective-permute-start.10
  233.5 4.7 %collective-permute-start.11 = (f32[1,1,128,128]{3,2,1,0:T(8,128)S(1)}, f32[1,1,128,128]{3,2,1,0:T(8,128)S(1)}, u32[]{:S(2)}, u32[]{:S(2)}) collective-permute-start(f32[1,1,128,128]{3,2,1,0:T(8,128)S(1)} %get-tuple-element.52), channel_id=1, source_target_pairs={{0,4},{4,8},{8,12},{12,16},{16,20},{20,24},{24,28},{1,5},{5,9},{9,... | collective-permute-start | bytes 196616 | tf_op jit(solution)/shard_map/ppermute | solution.py:17
  238.3 1.3 collective-permute-start.12
  239.6 4.9 %collective-permute-start.13 = (f32[1,1,64,64]{3,2,1,0:T(8,128)S(1)}, f32[1,1,64,64]{3,2,1,0:T(8,128)S(1)}, u32[]{:S(2)}, u32[]{:S(2)}) collective-permute-start(f32[1,1,64,64]{3,2,1,0:T(8,128)S(1)} %broadcast.208), channel_id=1, source_target_pairs={{0,4},{4,8},{8,12},{12,16},{16,20},{20,24},{24,28},{1,5},{5,9},{9,... | collective-permute-start | bytes 49160 | tf_op jit(solution)/shard_map/ppermute | solution.py:17
  244.7 18.1 %reshape.103 = f32[2,2,64,2,64,2]{5,4,3,2,1,0:T(8,128)} reshape(f32[1,4,128,128]{3,2,1,0:T(8,128)S(1)} %fusion.73) | data formatting | bytes 524288 | tf_op jit(solution)/shard_map/reshape | solution.py:48
  262.8 7.0 %reduce_sum.61 = f32[2,64,64]{2,1,0:T(8,128)S(1)} reduce(f32[2,2,64,2,64,2]{5,4,3,2,1,0:T(8,128)} %reshape.103, f32[]{:T(128)} %constant.30.clone.1), dimensions={1,3,5}, to_apply=%region_1.3 | reduce | flops 57344 | bytes 294916 | tf_op jit(solution)/shard_map/reduce_sum | solution.py:48
  270.0 1.3 collective-permute-start.14
  271.3 4.3 %collective-permute-start.15 = (f32[1,1,64,64]{3,2,1,0:T(8,128)S(1)}, f32[1,1,64,64]{3,2,1,0:T(8,128)S(1)}, u32[]{:S(2)}, u32[]{:S(2)}) collective-permute-start(f32[1,1,64,64]{3,2,1,0:T(8,128)S(1)} %get-tuple-element.64), channel_id=1, source_target_pairs={{0,4},{4,8},{8,12},{12,16},{16,20},{20,24},{24,28},{1,5},{5,9},{9,... | collective-permute-start | bytes 49160 | tf_op jit(solution)/shard_map/ppermute | solution.py:17
  276.5 1.3 collective-permute-start.16
  277.8 4.6 %collective-permute-start.17 = (f32[1,1,64,64]{3,2,1,0:T(8,128)S(1)}, f32[1,1,64,64]{3,2,1,0:T(8,128)S(1)}, u32[]{:S(2)}, u32[]{:S(2)}) collective-permute-start(f32[1,1,64,64]{3,2,1,0:T(8,128)S(1)} %get-tuple-element.62), channel_id=1, source_target_pairs={{0,4},{4,8},{8,12},{12,16},{16,20},{20,24},{24,28},{1,5},{5,9},{9,... | collective-permute-start | bytes 49160 | tf_op jit(solution)/shard_map/ppermute | solution.py:17
  283.8 1.8 reduce_sum.63
  285.9 17.4 %all-gather = f32[256,32]{1,0:T(8,128)S(1)} all-gather(f32[32,32]{1,0:T(8,128)S(1)} %broadcast_multiply_fusion.4), channel_id=2, replica_groups=mesh['gz'=8,'pair'=4] {'gz'}, dimensions={0}, use_global_device_ids=true | all-gather | bytes 36864 | tf_op jit(solution)/shard_map/all_gather | solution.py:56
  305.1 1.3 collective-permute-start.18
  306.4 3.0 collective-permute-start.19
  310.4 1.3 collective-permute-start.20
  311.7 4.3 %collective-permute-start.21 = (f32[1,1,64,64]{3,2,1,0:T(8,128)S(1)}, f32[1,1,64,64]{3,2,1,0:T(8,128)S(1)}, u32[]{:S(2)}, u32[]{:S(2)}) collective-permute-start(f32[1,1,64,64]{3,2,1,0:T(8,128)S(1)} %get-tuple-element.58), channel_id=1, source_target_pairs={{0,4},{4,8},{8,12},{12,16},{16,20},{20,24},{24,28},{1,5},{5,9},{9,... | collective-permute-start | bytes 49160 | tf_op jit(solution)/shard_map/ppermute | solution.py:17
  317.5 1.3 collective-permute-start.22
  318.8 5.0 %collective-permute-start.23 = (f32[1,1,128,128]{3,2,1,0:T(8,128)S(1)}, f32[1,1,128,128]{3,2,1,0:T(8,128)S(1)}, u32[]{:S(2)}, u32[]{:S(2)}) collective-permute-start(f32[1,1,128,128]{3,2,1,0:T(8,128)S(1)} %get-tuple-element.50), channel_id=1, source_target_pairs={{0,4},{4,8},{8,12},{12,16},{16,20},{20,24},{24,28},{1,5},{5,9},{9,... | collective-permute-start | bytes 196616 | tf_op jit(solution)/shard_map/ppermute | solution.py:17
  324.9 1.3 collective-permute-start.24
  326.2 5.3 %collective-permute-start.25 = (f32[1,1,128,128]{3,2,1,0:T(8,128)S(1)}, f32[1,1,128,128]{3,2,1,0:T(8,128)S(1)}, u32[]{:S(2)}, u32[]{:S(2)}) collective-permute-start(f32[1,1,128,128]{3,2,1,0:T(8,128)S(1)} %get-tuple-element.48), channel_id=1, source_target_pairs={{0,4},{4,8},{8,12},{12,16},{16,20},{20,24},{24,28},{1,5},{5,9},{9,... | collective-permute-start | bytes 196616 | tf_op jit(solution)/shard_map/ppermute | solution.py:17
  334.0 1.7 copy.43
  335.8 1.8 bitcast_add_fusion
  339.2 5.3 %collective-permute-start.27 = (f32[1,1,256,256]{2,1,3,0:T(1,128)S(1)}, f32[1,1,256,256]{2,1,3,0:T(1,128)S(1)}, u32[]{:S(2)}, u32[]{:S(2)}) collective-permute-start(f32[1,1,256,256]{2,1,3,0:T(1,128)S(1)} %get-tuple-element.42), channel_id=1, source_target_pairs={{0,4},{4,8},{8,12},{12,16},{16,20},{20,24},{24,28},{1,5},{5,9},{9,... | collective-permute-start | bytes 786440 | tf_op jit(solution)/shard_map/ppermute | solution.py:17
  345.7 2.2 fusion.28
  349.5 7.1 %collective-permute-start.29 = (f32[1,1,256,256]{2,1,3,0:T(1,128)S(1)}, f32[1,1,256,256]{2,1,3,0:T(1,128)S(1)}, u32[]{:S(2)}, u32[]{:S(2)}) collective-permute-start(f32[1,1,256,256]{2,1,3,0:T(1,128)S(1)} %get-tuple-element.40), channel_id=1, source_target_pairs={{0,4},{4,8},{8,12},{12,16},{16,20},{20,24},{24,28},{1,5},{5,9},{9,... | collective-permute-start | bytes 786440 | tf_op jit(solution)/shard_map/ppermute | solution.py:17
  357.7 2.2 fusion.36
  361.5 7.2 %collective-permute-start.31 = (f32[1,1,256,256]{2,1,3,0:T(1,128)S(1)}, f32[1,1,256,256]{2,1,3,0:T(1,128)S(1)}, u32[]{:S(2)}, u32[]{:S(2)}) collective-permute-start(f32[1,1,256,256]{2,1,3,0:T(1,128)S(1)} %get-tuple-element.38), channel_id=1, source_target_pairs={{0,4},{4,8},{8,12},{12,16},{16,20},{20,24},{24,28},{1,5},{5,9},{9,... | collective-permute-start | bytes 786440 | tf_op jit(solution)/shard_map/ppermute | solution.py:17
  369.8 2.9 multiply_reduce_fusion
  372.8 18.9 %all-reduce.30 = (f32[1]{0:T(128)}, f32[1]{0:T(128)}) all-reduce(f32[1]{0:T(128)} %bitcast.20, f32[1]{0:T(128)} %bitcast.21), channel_id=1, replica_groups=mesh['gz'=8,'pair'=4] {'gz'}, use_global_device_ids=true, to_apply=%region_5.7 | all-reduce | flops 2 | bytes 16 | tf_op jit(solution)/shard_map/psum | solution.py:90
  392.3 2.9 copy.44
  395.2 10.4 %psum.23 = f32[1]{0:T(128)} all-reduce(f32[1]{0:T(128)S(6)} %div.42), channel_id=1, replica_groups=mesh['gz'=8,'pair'=4] {'pair'}, use_global_device_ids=true, to_apply=%region_8.10 | all-reduce | flops 1 | bytes 8 | tf_op jit(solution)/shard_map/psum | solution.py:96
  (103 shorter events, 25.5 us)
Async XLA Ops:
  1.5 14.0 %collective-permute-start = (f32[1,1,256,256]{2,1,3,0:T(1,128)}, f32[1,1,256,256]{2,1,3,0:T(1,128)S(1)}, u32[]{:S(2)}, u32[]{:S(2)}) collective-permute-start(f32[1,1,256,256]{2,1,3,0:T(1,128)} %broadcast.199), channel_id=1, source_target_pairs={{4,0},{8,4},{12,8},{16,12},{20,16},{24,20},{28,24},{5,1},{9,5},{13... | collective-permute-start | bytes 786440 | tf_op jit(solution)/shard_map/ppermute | solution.py:20
  2.8 12.7 %collective-permute-start.1 = (f32[1,1,256,256]{2,1,3,0:T(1,128)}, f32[1,1,256,256]{2,1,3,0:T(1,128)}, u32[]{:S(2)}, u32[]{:S(2)}) collective-permute-start(f32[1,1,256,256]{2,1,3,0:T(1,128)} %broadcast.199), channel_id=1, source_target_pairs={{0,4},{4,8},{8,12},{12,16},{16,20},{20,24},{24,28},{1,5},{5,9},{9,... | collective-permute-start | bytes 786440 | tf_op jit(solution)/shard_map/ppermute | solution.py:17
  18.7 5.8 %collective-permute-start.2 = (f32[1,1,256,256]{2,1,3,0:T(1,128)S(1)}, f32[1,1,256,256]{2,1,3,0:T(1,128)S(1)}, u32[]{:S(2)}, u32[]{:S(2)}) collective-permute-start(f32[1,1,256,256]{2,1,3,0:T(1,128)S(1)} %get-tuple-element.45), channel_id=1, source_target_pairs={{4,0},{8,4},{12,8},{16,12},{20,16},{24,20},{28,24},{5,1},{9,5},{13... | collective-permute-start | bytes 786440 | tf_op jit(solution)/shard_map/ppermute | solution.py:20
  20.0 5.7 %collective-permute-start.3 = (f32[1,1,256,256]{2,1,3,0:T(1,128)S(1)}, f32[1,1,256,256]{2,1,3,0:T(1,128)S(1)}, u32[]{:S(2)}, u32[]{:S(2)}) collective-permute-start(f32[1,1,256,256]{2,1,3,0:T(1,128)S(1)} %get-tuple-element.46), channel_id=1, source_target_pairs={{0,4},{4,8},{8,12},{12,16},{16,20},{20,24},{24,28},{1,5},{5,9},{9,... | collective-permute-start | bytes 786440 | tf_op jit(solution)/shard_map/ppermute | solution.py:17
  28.0 14.4 %copy-start = (f32[1,8,256,256]{2,1,3,0:T(8,128)}, f32[1,8,256,256]{2,1,3,0:T(8,128)S(1)}, u32[]{:S(2)}) copy-start(f32[1,8,256,256]{2,1,3,0:T(8,128)S(1)} %fusion.14) | copy-start | bytes 6291460
  28.3 14.1 %collective-permute-start.4 = (f32[1,1,256,256]{2,1,3,0:T(1,128)S(1)}, f32[1,1,256,256]{2,1,3,0:T(1,128)S(1)}, u32[]{:S(2)}, u32[]{:S(2)}) collective-permute-start(f32[1,1,256,256]{2,1,3,0:T(1,128)S(1)} %get-tuple-element.43), channel_id=1, source_target_pairs={{4,0},{8,4},{12,8},{16,12},{20,16},{24,20},{28,24},{5,1},{9,5},{13... | collective-permute-start | bytes 786440 | tf_op jit(solution)/shard_map/ppermute | solution.py:20
  29.6 12.8 %collective-permute-start.5 = (f32[1,1,256,256]{2,1,3,0:T(1,128)S(1)}, f32[1,1,256,256]{2,1,3,0:T(1,128)S(1)}, u32[]{:S(2)}, u32[]{:S(2)}) collective-permute-start(f32[1,1,256,256]{2,1,3,0:T(1,128)S(1)} %get-tuple-element.44), channel_id=1, source_target_pairs={{0,4},{4,8},{8,12},{12,16},{16,20},{20,24},{24,28},{1,5},{5,9},{9,... | collective-permute-start | bytes 786440 | tf_op jit(solution)/shard_map/ppermute | solution.py:17
  36.1 189.2 %collective-permute-start.6 = (f32[1,1,128,128]{3,2,1,0:T(8,128)S(1)}, f32[1,1,128,128]{3,2,1,0:T(8,128)S(1)}, u32[]{:S(2)}, u32[]{:S(2)}) collective-permute-start(f32[1,1,128,128]{3,2,1,0:T(8,128)S(1)} %broadcast.203), channel_id=1, source_target_pairs={{4,0},{8,4},{12,8},{16,12},{20,16},{24,20},{28,24},{5,1},{9,5},{13... | collective-permute-start | bytes 196616 | tf_op jit(solution)/shard_map/ppermute | solution.py:20
  37.4 187.9 %collective-permute-start.7 = (f32[1,1,128,128]{3,2,1,0:T(8,128)S(1)}, f32[1,1,128,128]{3,2,1,0:T(8,128)S(1)}, u32[]{:S(2)}, u32[]{:S(2)}) collective-permute-start(f32[1,1,128,128]{3,2,1,0:T(8,128)S(1)} %broadcast.203), channel_id=1, source_target_pairs={{0,4},{4,8},{8,12},{12,16},{16,20},{20,24},{24,28},{1,5},{5,9},{9,... | collective-permute-start | bytes 196616 | tf_op jit(solution)/shard_map/ppermute | solution.py:17
  225.5 5.6 %collective-permute-start.8 = (f32[1,1,128,128]{3,2,1,0:T(8,128)S(1)}, f32[1,1,128,128]{3,2,1,0:T(8,128)S(1)}, u32[]{:S(2)}, u32[]{:S(2)}) collective-permute-start(f32[1,1,128,128]{3,2,1,0:T(8,128)S(1)} %get-tuple-element.53), channel_id=1, source_target_pairs={{4,0},{8,4},{12,8},{16,12},{20,16},{24,20},{28,24},{5,1},{9,5},{13... | collective-permute-start | bytes 196616 | tf_op jit(solution)/shard_map/ppermute | solution.py:20
  226.8 5.2 %collective-permute-start.9 = (f32[1,1,128,128]{3,2,1,0:T(8,128)S(1)}, f32[1,1,128,128]{3,2,1,0:T(8,128)S(1)}, u32[]{:S(2)}, u32[]{:S(2)}) collective-permute-start(f32[1,1,128,128]{3,2,1,0:T(8,128)S(1)} %get-tuple-element.54), channel_id=1, source_target_pairs={{0,4},{4,8},{8,12},{12,16},{16,20},{20,24},{24,28},{1,5},{5,9},{9,... | collective-permute-start | bytes 196616 | tf_op jit(solution)/shard_map/ppermute | solution.py:17
  232.2 12.3 %copy-start.2 = (f32[1,4,128,128]{3,2,1,0:T(8,128)}, f32[1,4,128,128]{3,2,1,0:T(8,128)S(1)}, u32[]{:S(2)}) copy-start(f32[1,4,128,128]{3,2,1,0:T(8,128)S(1)} %fusion.66) | copy-start | bytes 786436
  232.2 12.2 %collective-permute-start.10 = (f32[1,1,128,128]{3,2,1,0:T(8,128)S(1)}, f32[1,1,128,128]{3,2,1,0:T(8,128)S(1)}, u32[]{:S(2)}, u32[]{:S(2)}) collective-permute-start(f32[1,1,128,128]{3,2,1,0:T(8,128)S(1)} %get-tuple-element.51), channel_id=1, source_target_pairs={{4,0},{8,4},{12,8},{16,12},{20,16},{24,20},{28,24},{5,1},{9,5},{13... | collective-permute-start | bytes 196616 | tf_op jit(solution)/shard_map/ppermute | solution.py:20
  233.5 10.9 %collective-permute-start.11 = (f32[1,1,128,128]{3,2,1,0:T(8,128)S(1)}, f32[1,1,128,128]{3,2,1,0:T(8,128)S(1)}, u32[]{:S(2)}, u32[]{:S(2)}) collective-permute-start(f32[1,1,128,128]{3,2,1,0:T(8,128)S(1)} %get-tuple-element.52), channel_id=1, source_target_pairs={{0,4},{4,8},{8,12},{12,16},{16,20},{20,24},{24,28},{1,5},{5,9},{9,... | collective-permute-start | bytes 196616 | tf_op jit(solution)/shard_map/ppermute | solution.py:17
  238.3 31.5 %collective-permute-start.12 = (f32[1,1,64,64]{3,2,1,0:T(8,128)S(1)}, f32[1,1,64,64]{3,2,1,0:T(8,128)S(1)}, u32[]{:S(2)}, u32[]{:S(2)}) collective-permute-start(f32[1,1,64,64]{3,2,1,0:T(8,128)S(1)} %broadcast.208), channel_id=1, source_target_pairs={{4,0},{8,4},{12,8},{16,12},{20,16},{24,20},{28,24},{5,1},{9,5},{13... | collective-permute-start | bytes 49160 | tf_op jit(solution)/shard_map/ppermute | solution.py:20
  239.6 30.2 %collective-permute-start.13 = (f32[1,1,64,64]{3,2,1,0:T(8,128)S(1)}, f32[1,1,64,64]{3,2,1,0:T(8,128)S(1)}, u32[]{:S(2)}, u32[]{:S(2)}) collective-permute-start(f32[1,1,64,64]{3,2,1,0:T(8,128)S(1)} %broadcast.208), channel_id=1, source_target_pairs={{0,4},{4,8},{8,12},{12,16},{16,20},{20,24},{24,28},{1,5},{5,9},{9,... | collective-permute-start | bytes 49160 | tf_op jit(solution)/shard_map/ppermute | solution.py:17
  270.0 5.6 %collective-permute-start.14 = (f32[1,1,64,64]{3,2,1,0:T(8,128)S(1)}, f32[1,1,64,64]{3,2,1,0:T(8,128)S(1)}, u32[]{:S(2)}, u32[]{:S(2)}) collective-permute-start(f32[1,1,64,64]{3,2,1,0:T(8,128)S(1)} %get-tuple-element.63), channel_id=1, source_target_pairs={{4,0},{8,4},{12,8},{16,12},{20,16},{24,20},{28,24},{5,1},{9,5},{13... | collective-permute-start | bytes 49160 | tf_op jit(solution)/shard_map/ppermute | solution.py:20
  271.3 5.1 %collective-permute-start.15 = (f32[1,1,64,64]{3,2,1,0:T(8,128)S(1)}, f32[1,1,64,64]{3,2,1,0:T(8,128)S(1)}, u32[]{:S(2)}, u32[]{:S(2)}) collective-permute-start(f32[1,1,64,64]{3,2,1,0:T(8,128)S(1)} %get-tuple-element.64), channel_id=1, source_target_pairs={{0,4},{4,8},{8,12},{12,16},{16,20},{20,24},{24,28},{1,5},{5,9},{9,... | collective-permute-start | bytes 49160 | tf_op jit(solution)/shard_map/ppermute | solution.py:17
  276.5 5.9 %collective-permute-start.16 = (f32[1,1,64,64]{3,2,1,0:T(8,128)S(1)}, f32[1,1,64,64]{3,2,1,0:T(8,128)S(1)}, u32[]{:S(2)}, u32[]{:S(2)}) collective-permute-start(f32[1,1,64,64]{3,2,1,0:T(8,128)S(1)} %get-tuple-element.61), channel_id=1, source_target_pairs={{4,0},{8,4},{12,8},{16,12},{20,16},{24,20},{28,24},{5,1},{9,5},{13... | collective-permute-start | bytes 49160 | tf_op jit(solution)/shard_map/ppermute | solution.py:20
  277.8 5.3 %collective-permute-start.17 = (f32[1,1,64,64]{3,2,1,0:T(8,128)S(1)}, f32[1,1,64,64]{3,2,1,0:T(8,128)S(1)}, u32[]{:S(2)}, u32[]{:S(2)}) collective-permute-start(f32[1,1,64,64]{3,2,1,0:T(8,128)S(1)} %get-tuple-element.62), channel_id=1, source_target_pairs={{0,4},{4,8},{8,12},{12,16},{16,20},{20,24},{24,28},{1,5},{5,9},{9,... | collective-permute-start | bytes 49160 | tf_op jit(solution)/shard_map/ppermute | solution.py:17
  304.2 13.2 %copy-start.3 = (f32[1,4,128,128]{3,2,1,0:T(8,128)S(1)}, f32[1,4,128,128]{3,2,1,0:T(8,128)}, u32[]{:S(2)}) copy-start(f32[1,4,128,128]{3,2,1,0:T(8,128)} %copy-done.2) | copy-start | bytes 786436
  305.1 4.3 %collective-permute-start.18 = (f32[1,1,64,64]{3,2,1,0:T(8,128)S(1)}, f32[1,1,64,64]{3,2,1,0:T(8,128)S(1)}, u32[]{:S(2)}, u32[]{:S(2)}) collective-permute-start(f32[1,1,64,64]{3,2,1,0:T(8,128)S(1)} %get-tuple-element.59), channel_id=1, source_target_pairs={{4,0},{8,4},{12,8},{16,12},{20,16},{24,20},{28,24},{5,1},{9,5},{13... | collective-permute-start | bytes 49160 | tf_op jit(solution)/shard_map/ppermute | solution.py:20
  306.4 3.9 collective-permute-start.19
  310.4 5.6 %collective-permute-start.20 = (f32[1,1,64,64]{3,2,1,0:T(8,128)S(1)}, f32[1,1,64,64]{3,2,1,0:T(8,128)S(1)}, u32[]{:S(2)}, u32[]{:S(2)}) collective-permute-start(f32[1,1,64,64]{3,2,1,0:T(8,128)S(1)} %get-tuple-element.57), channel_id=1, source_target_pairs={{4,0},{8,4},{12,8},{16,12},{20,16},{24,20},{28,24},{5,1},{9,5},{13... | collective-permute-start | bytes 49160 | tf_op jit(solution)/shard_map/ppermute | solution.py:20
  311.7 5.1 %collective-permute-start.21 = (f32[1,1,64,64]{3,2,1,0:T(8,128)S(1)}, f32[1,1,64,64]{3,2,1,0:T(8,128)S(1)}, u32[]{:S(2)}, u32[]{:S(2)}) collective-permute-start(f32[1,1,64,64]{3,2,1,0:T(8,128)S(1)} %get-tuple-element.58), channel_id=1, source_target_pairs={{0,4},{4,8},{8,12},{12,16},{16,20},{20,24},{24,28},{1,5},{5,9},{9,... | collective-permute-start | bytes 49160 | tf_op jit(solution)/shard_map/ppermute | solution.py:17
  317.5 6.3 %collective-permute-start.22 = (f32[1,1,128,128]{3,2,1,0:T(8,128)S(1)}, f32[1,1,128,128]{3,2,1,0:T(8,128)S(1)}, u32[]{:S(2)}, u32[]{:S(2)}) collective-permute-start(f32[1,1,128,128]{3,2,1,0:T(8,128)S(1)} %get-tuple-element.49), channel_id=1, source_target_pairs={{4,0},{8,4},{12,8},{16,12},{20,16},{24,20},{28,24},{5,1},{9,5},{13... | collective-permute-start | bytes 196616 | tf_op jit(solution)/shard_map/ppermute | solution.py:20
  318.8 5.9 %collective-permute-start.23 = (f32[1,1,128,128]{3,2,1,0:T(8,128)S(1)}, f32[1,1,128,128]{3,2,1,0:T(8,128)S(1)}, u32[]{:S(2)}, u32[]{:S(2)}) collective-permute-start(f32[1,1,128,128]{3,2,1,0:T(8,128)S(1)} %get-tuple-element.50), channel_id=1, source_target_pairs={{0,4},{4,8},{8,12},{12,16},{16,20},{20,24},{24,28},{1,5},{5,9},{9,... | collective-permute-start | bytes 196616 | tf_op jit(solution)/shard_map/ppermute | solution.py:17
  324.9 6.6 %collective-permute-start.24 = (f32[1,1,128,128]{3,2,1,0:T(8,128)S(1)}, f32[1,1,128,128]{3,2,1,0:T(8,128)S(1)}, u32[]{:S(2)}, u32[]{:S(2)}) collective-permute-start(f32[1,1,128,128]{3,2,1,0:T(8,128)S(1)} %get-tuple-element.47), channel_id=1, source_target_pairs={{4,0},{8,4},{12,8},{16,12},{20,16},{24,20},{28,24},{5,1},{9,5},{13... | collective-permute-start | bytes 196616 | tf_op jit(solution)/shard_map/ppermute | solution.py:20
  326.2 6.2 %collective-permute-start.25 = (f32[1,1,128,128]{3,2,1,0:T(8,128)S(1)}, f32[1,1,128,128]{3,2,1,0:T(8,128)S(1)}, u32[]{:S(2)}, u32[]{:S(2)}) collective-permute-start(f32[1,1,128,128]{3,2,1,0:T(8,128)S(1)} %get-tuple-element.48), channel_id=1, source_target_pairs={{0,4},{4,8},{8,12},{12,16},{16,20},{20,24},{24,28},{1,5},{5,9},{9,... | collective-permute-start | bytes 196616 | tf_op jit(solution)/shard_map/ppermute | solution.py:17
  337.9 6.6 %collective-permute-start.26 = (f32[1,1,256,256]{2,1,3,0:T(1,128)S(1)}, f32[1,1,256,256]{2,1,3,0:T(1,128)S(1)}, u32[]{:S(2)}, u32[]{:S(2)}) collective-permute-start(f32[1,1,256,256]{2,1,3,0:T(1,128)S(1)} %get-tuple-element.41), channel_id=1, source_target_pairs={{4,0},{8,4},{12,8},{16,12},{20,16},{24,20},{28,24},{5,1},{9,5},{13... | collective-permute-start | bytes 786440 | tf_op jit(solution)/shard_map/ppermute | solution.py:20
  339.2 6.5 %collective-permute-start.27 = (f32[1,1,256,256]{2,1,3,0:T(1,128)S(1)}, f32[1,1,256,256]{2,1,3,0:T(1,128)S(1)}, u32[]{:S(2)}, u32[]{:S(2)}) collective-permute-start(f32[1,1,256,256]{2,1,3,0:T(1,128)S(1)} %get-tuple-element.42), channel_id=1, source_target_pairs={{0,4},{4,8},{8,12},{12,16},{16,20},{20,24},{24,28},{1,5},{5,9},{9,... | collective-permute-start | bytes 786440 | tf_op jit(solution)/shard_map/ppermute | solution.py:17
  348.2 8.4 %collective-permute-start.28 = (f32[1,1,256,256]{2,1,3,0:T(1,128)S(1)}, f32[1,1,256,256]{2,1,3,0:T(1,128)S(1)}, u32[]{:S(2)}, u32[]{:S(2)}) collective-permute-start(f32[1,1,256,256]{2,1,3,0:T(1,128)S(1)} %get-tuple-element.39), channel_id=1, source_target_pairs={{4,0},{8,4},{12,8},{16,12},{20,16},{24,20},{28,24},{5,1},{9,5},{13... | collective-permute-start | bytes 786440 | tf_op jit(solution)/shard_map/ppermute | solution.py:20
  349.5 8.2 %collective-permute-start.29 = (f32[1,1,256,256]{2,1,3,0:T(1,128)S(1)}, f32[1,1,256,256]{2,1,3,0:T(1,128)S(1)}, u32[]{:S(2)}, u32[]{:S(2)}) collective-permute-start(f32[1,1,256,256]{2,1,3,0:T(1,128)S(1)} %get-tuple-element.40), channel_id=1, source_target_pairs={{0,4},{4,8},{8,12},{12,16},{16,20},{20,24},{24,28},{1,5},{5,9},{9,... | collective-permute-start | bytes 786440 | tf_op jit(solution)/shard_map/ppermute | solution.py:17
  359.9 12.9 %copy-start.1 = (f32[1,8,256,256]{2,1,3,0:T(8,128)}, f32[1,8,256,256]{2,1,3,0:T(8,128)S(1)}, u32[]{:S(2)}) copy-start(f32[1,8,256,256]{2,1,3,0:T(8,128)S(1)} %fusion.36) | copy-start | bytes 6291460
  360.2 9.1 %collective-permute-start.30 = (f32[1,1,256,256]{2,1,3,0:T(1,128)S(1)}, f32[1,1,256,256]{2,1,3,0:T(1,128)S(1)}, u32[]{:S(2)}, u32[]{:S(2)}) collective-permute-start(f32[1,1,256,256]{2,1,3,0:T(1,128)S(1)} %get-tuple-element.37), channel_id=1, source_target_pairs={{4,0},{8,4},{12,8},{16,12},{20,16},{24,20},{28,24},{5,1},{9,5},{13... | collective-permute-start | bytes 786440 | tf_op jit(solution)/shard_map/ppermute | solution.py:20
  361.5 8.3 %collective-permute-start.31 = (f32[1,1,256,256]{2,1,3,0:T(1,128)S(1)}, f32[1,1,256,256]{2,1,3,0:T(1,128)S(1)}, u32[]{:S(2)}, u32[]{:S(2)}) collective-permute-start(f32[1,1,256,256]{2,1,3,0:T(1,128)S(1)} %get-tuple-element.38), channel_id=1, source_target_pairs={{0,4},{4,8},{8,12},{12,16},{16,20},{20,24},{24,28},{1,5},{5,9},{9,... | collective-permute-start | bytes 786440 | tf_op jit(solution)/shard_map/ppermute | solution.py:17
where the time goes:
time: 409 us; the launch traced here: 407 us
  local copies, waits for them, and re-layouts  174 us (43%)
  starting transfers between devices  100 us (24%)
  other arithmetic  68.6 us (17%)
  blocking collectives  46.6 us (11%)
  waiting for transfers between devices  9.63 us (2%)
  between operations  8.59 us (2%)
    reshape x2, local copies, waits for them, and re-layouts, restrict(): field.reshape(pairs, zsize // 2, 2, ysize // 2, 2, xsize // 2, 2)  154 us
    ppermute x16, starting transfers between devices, with_halo(): lax.ppermute(lax.slice_in_dim(block, block.shape[dim] - width, None, axis...  79.6 us
    reduce_sum x4, other arithmetic, restrict(): field.reshape(pairs, zsize // 2, 2, ysize // 2, 2, xsize // 2, 2)  48.5 us
    ppermute x16, starting transfers between devices, with_halo(): lax.ppermute(lax.slice_in_dim(block, 0, width, axis=dim), axis, backward)  20.7 us
    psum x1, blocking collectives, per_device(): lax.psum((jnp.sum(final * final, axis=(1, 2, 3)), jnp.sum(density * poten...  18.9 us
    all_gather x1, blocking collectives, coarsest(): gathered = lax.all_gather(source, 'gz', axis=1, tiled=True)  17.4 us
    psum x1, blocking collectives, per_device(): energy = lax.psum(partial_energy, 'pair').reshape(1)  10.4 us
    ppermute x16, waiting for transfers between devices, with_halo(): lax.ppermute(lax.slice_in_dim(block, block.shape[dim] - width, None, axis...  9.58 us
  transfers between devices with their start and end apart: 32, of which 11 were waited for; matrix products, arithmetic and copies ran while one was open for 52% of the time, Pallas kernels for 0%

commit v1 on v0

--- a/solution.py
+++ b/solution.py
@@ -93,7 +93,7 @@
     cell_count = density.shape[1] * lax.axis_size("gz") * density.shape[2] * density.shape[3]
     residual_norm = jnp.sqrt(totals[0] / cell_count)
     partial_energy = -0.5 * jnp.sum(pair_weight * totals[1]) / cell_count
-    energy = lax.psum(partial_energy, "pair").reshape(1)
+    energy = jnp.sum(lax.all_gather(partial_energy, "pair"), axis=0).reshape(1)
     return (potential, residual_norm, energy)
 
 

time: 409 us -> 417 us (1.020)
  other arithmetic: 68.6 us -> 76.7 us
    psum x1 -> x0, blocking collectives: 10.4 us -> none  [per_device(): energy = lax.psum(partial_energy, 'pair').reshape(1)]
    unnamed x0 -> x1, blocking collectives: none -> 9.88 us
    reduce_sum x1, other arithmetic: 2.94 us -> 9.01 us  [per_device(): jnp.sum(density * potential, axis=(1, 2, 3))]
  transfers between devices with their start and end apart: 32 -> 32, of which waited for: 11 -> 10; matrix products, arithmetic and copies ran while one was open for 52% -> 51% of each run, Pallas kernels for 0% -> 0%
where the time goes in v1:
time: 417 us; the launch traced here: 416 us
  local copies, waits for them, and re-layouts  176 us (42%)
  starting transfers between devices  100 us (24%)
  other arithmetic  76.7 us (18%)
  blocking collectives  45.9 us (11%)
  waiting for transfers between devices  9.16 us (2%)
  between operations  7.95 us (2%)
    reshape x2, local copies, waits for them, and re-layouts, restrict(): field.reshape(pairs, zsize // 2, 2, ysize // 2, 2, xsize // 2, 2)  154 us
    ppermute x16, starting transfers between devices, with_halo(): lax.ppermute(lax.slice_in_dim(block, block.shape[dim] - width, None, axis...  79.6 us
    reduce_sum x4, other arithmetic, restrict(): field.reshape(pairs, zsize // 2, 2, ysize // 2, 2, xsize // 2, 2)  48.5 us
    ppermute x16, starting transfers between devices, with_halo(): lax.ppermute(lax.slice_in_dim(block, 0, width, axis=dim), axis, backward)  20.7 us
    psum x1, blocking collectives, per_device(): lax.psum((jnp.sum(final * final, axis=(1, 2, 3)), jnp.sum(density * poten...  18.7 us
    all_gather x1, blocking collectives, coarsest(): gathered = lax.all_gather(source, 'gz', axis=1, tiled=True)  17.4 us
    unnamed x1, blocking collectives  9.88 us
    ppermute x16, waiting for transfers between devices, with_halo(): lax.ppermute(lax.slice_in_dim(block, block.shape[dim] - width, None, axis...  9.11 us
  transfers between devices with their start and end apart: 32, of which 10 were waited for; matrix products, arithmetic and copies ran while one was open for 51% of the time, Pallas kernels for 0%

profile of v1, /device:TPU:0, one launch (start us, length us, event | category | flops | bytes accessed | tf_op | source)
XLA Modules:
  0.0 415.7 jit_solution(14362446712703342468)
XLA Ops:
  2.8 3.7 collective-permute-start.1
  6.5 1.3 fusion.235
  11.7 1.7 constant_dynamic-slice_fusion.1
  15.6 2.7 broadcast_multiply_fusion
  18.7 1.3 collective-permute-start.2
  20.0 4.5 %collective-permute-start.3 = (f32[1,1,256,256]{2,1,3,0:T(1,128)S(1)}, f32[1,1,256,256]{2,1,3,0:T(1,128)S(1)}, u32[]{:S(2)}, u32[]{:S(2)}) collective-permute-start(f32[1,1,256,256]{2,1,3,0:T(1,128)S(1)} %get-tuple-element.46), channel_id=1, source_target_pairs={{0,4},{4,8},{8,12},{12,16},{16,20},{20,24},{24,28},{1,5},{5,9},{9,... | collective-permute-start | bytes 786440 | tf_op jit(solution)/shard_map/ppermute | solution.py:17
  25.7 2.3 fusion.14
  28.3 1.3 collective-permute-start.4
  29.6 6.4 %collective-permute-start.5 = (f32[1,1,256,256]{2,1,3,0:T(1,128)S(1)}, f32[1,1,256,256]{2,1,3,0:T(1,128)S(1)}, u32[]{:S(2)}, u32[]{:S(2)}) collective-permute-start(f32[1,1,256,256]{2,1,3,0:T(1,128)S(1)} %get-tuple-element.44), channel_id=1, source_target_pairs={{0,4},{4,8},{8,12},{12,16},{16,20},{20,24},{24,28},{1,5},{5,9},{9,... | collective-permute-start | bytes 786440 | tf_op jit(solution)/shard_map/ppermute | solution.py:17
  36.1 1.3 collective-permute-start.6
  37.4 5.0 %collective-permute-start.7 = (f32[1,1,128,128]{3,2,1,0:T(8,128)S(1)}, f32[1,1,128,128]{3,2,1,0:T(8,128)S(1)}, u32[]{:S(2)}, u32[]{:S(2)}) collective-permute-start(f32[1,1,128,128]{3,2,1,0:T(8,128)S(1)} %broadcast.203), channel_id=1, source_target_pairs={{0,4},{4,8},{8,12},{12,16},{16,20},{20,24},{24,28},{1,5},{5,9},{9,... | collective-permute-start | bytes 196616 | tf_op jit(solution)/shard_map/ppermute | solution.py:17
  42.4 3.0 fusion.20
  45.5 3.0 copy.35
  48.4 136.2 %reshape.103 = f32[4,2,128,2,128,2]{5,4,3,2,1,0:T(8,128)} reshape(f32[1,8,256,256]{3,2,1,0:T(8,128)} %copy.35) | data formatting | bytes 4194304 | tf_op jit(solution)/shard_map/reshape | solution.py:48
  184.6 40.6 %reduce_sum.69 = f32[4,128,128]{2,1,0:T(8,128)S(1)} reduce(f32[4,2,128,2,128,2]{5,4,3,2,1,0:T(8,128)} %reshape.103, f32[]{:T(128)} %constant.30.clone.1), dimensions={1,3,5}, to_apply=%region_0.0 | reduce | flops 458752 | bytes 2359300 | tf_op jit(solution)/shard_map/reduce_sum | solution.py:48
  226.8 4.3 %collective-permute-start.9 = (f32[1,1,128,128]{3,2,1,0:T(8,128)S(1)}, f32[1,1,128,128]{3,2,1,0:T(8,128)S(1)}, u32[]{:S(2)}, u32[]{:S(2)}) collective-permute-start(f32[1,1,128,128]{3,2,1,0:T(8,128)S(1)} %get-tuple-element.54), channel_id=1, source_target_pairs={{0,4},{4,8},{8,12},{12,16},{16,20},{20,24},{24,28},{1,5},{5,9},{9,... | collective-permute-start | bytes 196616 | tf_op jit(solution)/shard_map/ppermute | solution.py:17
  233.5 4.7 %collective-permute-start.11 = (f32[1,1,128,128]{3,2,1,0:T(8,128)S(1)}, f32[1,1,128,128]{3,2,1,0:T(8,128)S(1)}, u32[]{:S(2)}, u32[]{:S(2)}) collective-permute-start(f32[1,1,128,128]{3,2,1,0:T(8,128)S(1)} %get-tuple-element.52), channel_id=1, source_target_pairs={{0,4},{4,8},{8,12},{12,16},{16,20},{20,24},{24,28},{1,5},{5,9},{9,... | collective-permute-start | bytes 196616 | tf_op jit(solution)/shard_map/ppermute | solution.py:17
  239.5 4.9 %collective-permute-start.13 = (f32[1,1,64,64]{3,2,1,0:T(8,128)S(1)}, f32[1,1,64,64]{3,2,1,0:T(8,128)S(1)}, u32[]{:S(2)}, u32[]{:S(2)}) collective-permute-start(f32[1,1,64,64]{3,2,1,0:T(8,128)S(1)} %broadcast.208), channel_id=1, source_target_pairs={{0,4},{4,8},{8,12},{12,16},{16,20},{20,24},{24,28},{1,5},{5,9},{9,... | collective-permute-start | bytes 49160 | tf_op jit(solution)/shard_map/ppermute | solution.py:17
  244.7 18.1 %reshape.104 = f32[2,2,64,2,64,2]{5,4,3,2,1,0:T(8,128)} reshape(f32[1,4,128,128]{3,2,1,0:T(8,128)S(1)} %fusion.73) | data formatting | bytes 524288 | tf_op jit(solution)/shard_map/reshape | solution.py:48
  262.8 7.0 %reduce_sum.70 = f32[2,64,64]{2,1,0:T(8,128)S(1)} reduce(f32[2,2,64,2,64,2]{5,4,3,2,1,0:T(8,128)} %reshape.104, f32[]{:T(128)} %constant.30.clone.1), dimensions={1,3,5}, to_apply=%region_1.3 | reduce | flops 57344 | bytes 294916 | tf_op jit(solution)/shard_map/reduce_sum | solution.py:48
  269.9 1.3 collective-permute-start.14
  271.2 4.3 %collective-permute-start.15 = (f32[1,1,64,64]{3,2,1,0:T(8,128)S(1)}, f32[1,1,64,64]{3,2,1,0:T(8,128)S(1)}, u32[]{:S(2)}, u32[]{:S(2)}) collective-permute-start(f32[1,1,64,64]{3,2,1,0:T(8,128)S(1)} %get-tuple-element.64), channel_id=1, source_target_pairs={{0,4},{4,8},{8,12},{12,16},{16,20},{20,24},{24,28},{1,5},{5,9},{9,... | collective-permute-start | bytes 49160 | tf_op jit(solution)/shard_map/ppermute | solution.py:17
  277.8 4.6 %collective-permute-start.17 = (f32[1,1,64,64]{3,2,1,0:T(8,128)S(1)}, f32[1,1,64,64]{3,2,1,0:T(8,128)S(1)}, u32[]{:S(2)}, u32[]{:S(2)}) collective-permute-start(f32[1,1,64,64]{3,2,1,0:T(8,128)S(1)} %get-tuple-element.62), channel_id=1, source_target_pairs={{0,4},{4,8},{8,12},{12,16},{16,20},{20,24},{24,28},{1,5},{5,9},{9,... | collective-permute-start | bytes 49160 | tf_op jit(solution)/shard_map/ppermute | solution.py:17
  283.8 1.8 reduce_sum.72
  285.9 17.4 %all-gather = f32[256,32]{1,0:T(8,128)S(1)} all-gather(f32[32,32]{1,0:T(8,128)S(1)} %broadcast_multiply_fusion.4), channel_id=2, replica_groups=mesh['gz'=8,'pair'=4] {'gz'}, dimensions={0}, use_global_device_ids=true | all-gather | bytes 36864 | tf_op jit(solution)/shard_map/all_gather | solution.py:56
  305.0 1.3 collective-permute-start.18
  306.3 3.0 collective-permute-start.19
  310.4 1.3 collective-permute-start.20
  311.7 4.3 %collective-permute-start.21 = (f32[1,1,64,64]{3,2,1,0:T(8,128)S(1)}, f32[1,1,64,64]{3,2,1,0:T(8,128)S(1)}, u32[]{:S(2)}, u32[]{:S(2)}) collective-permute-start(f32[1,1,64,64]{3,2,1,0:T(8,128)S(1)} %get-tuple-element.58), channel_id=1, source_target_pairs={{0,4},{4,8},{8,12},{12,16},{16,20},{20,24},{24,28},{1,5},{5,9},{9,... | collective-permute-start | bytes 49160 | tf_op jit(solution)/shard_map/ppermute | solution.py:17
  317.4 1.3 collective-permute-start.22
  318.7 5.0 %collective-permute-start.23 = (f32[1,1,128,128]{3,2,1,0:T(8,128)S(1)}, f32[1,1,128,128]{3,2,1,0:T(8,128)S(1)}, u32[]{:S(2)}, u32[]{:S(2)}) collective-permute-start(f32[1,1,128,128]{3,2,1,0:T(8,128)S(1)} %get-tuple-element.50), channel_id=1, source_target_pairs={{0,4},{4,8},{8,12},{12,16},{16,20},{20,24},{24,28},{1,5},{5,9},{9,... | collective-permute-start | bytes 196616 | tf_op jit(solution)/shard_map/ppermute | solution.py:17
  326.2 5.3 %collective-permute-start.25 = (f32[1,1,128,128]{3,2,1,0:T(8,128)S(1)}, f32[1,1,128,128]{3,2,1,0:T(8,128)S(1)}, u32[]{:S(2)}, u32[]{:S(2)}) collective-permute-start(f32[1,1,128,128]{3,2,1,0:T(8,128)S(1)} %get-tuple-element.48), channel_id=1, source_target_pairs={{0,4},{4,8},{8,12},{12,16},{16,20},{20,24},{24,28},{1,5},{5,9},{9,... | collective-permute-start | bytes 196616 | tf_op jit(solution)/shard_map/ppermute | solution.py:17
  334.0 1.7 copy.43
  335.7 1.8 bitcast_add_fusion
  337.9 1.3 collective-permute-start.26
  339.2 5.3 %collective-permute-start.27 = (f32[1,1,256,256]{2,1,3,0:T(1,128)S(1)}, f32[1,1,256,256]{2,1,3,0:T(1,128)S(1)}, u32[]{:S(2)}, u32[]{:S(2)}) collective-permute-start(f32[1,1,256,256]{2,1,3,0:T(1,128)S(1)} %get-tuple-element.42), channel_id=1, source_target_pairs={{0,4},{4,8},{8,12},{12,16},{16,20},{20,24},{24,28},{1,5},{5,9},{9,... | collective-permute-start | bytes 786440 | tf_op jit(solution)/shard_map/ppermute | solution.py:17
  345.6 2.2 fusion.28
  348.2 1.3 collective-permute-start.28
  349.5 7.1 %collective-permute-start.29 = (f32[1,1,256,256]{2,1,3,0:T(1,128)S(1)}, f32[1,1,256,256]{2,1,3,0:T(1,128)S(1)}, u32[]{:S(2)}, u32[]{:S(2)}) collective-permute-start(f32[1,1,256,256]{2,1,3,0:T(1,128)S(1)} %get-tuple-element.40), channel_id=1, source_target_pairs={{0,4},{4,8},{8,12},{12,16},{16,20},{20,24},{24,28},{1,5},{5,9},{9,... | collective-permute-start | bytes 786440 | tf_op jit(solution)/shard_map/ppermute | solution.py:17
  357.7 2.2 fusion.36
  359.9 1.3 copy-done.1
  361.5 1.3 collective-permute-start.30
  362.8 7.2 %collective-permute-start.31 = (f32[1,1,256,256]{2,1,3,0:T(1,128)S(1)}, f32[1,1,256,256]{2,1,3,0:T(1,128)S(1)}, u32[]{:S(2)}, u32[]{:S(2)}) collective-permute-start(f32[1,1,256,256]{2,1,3,0:T(1,128)S(1)} %get-tuple-element.38), channel_id=1, source_target_pairs={{0,4},{4,8},{8,12},{12,16},{16,20},{20,24},{24,28},{1,5},{5,9},{9,... | collective-permute-start | bytes 786440 | tf_op jit(solution)/shard_map/ppermute | solution.py:17
  371.4 9.0 %multiply_reduce_fusion = (f32[]{:T(128)}, f32[]{:T(128)}) fusion(f32[1,8,256,256]{2,1,3,0:T(8,128)} %copy-done.1, bf16[1,8,256,256]{2,1,3,0:T(8,128)(2,1)S(1)} %copy.46, pred[]{:T(512)} %bitcast.1, bf16[1,8,256,256]{2,1,3,0:T(8,128)(2,1)S(1)} %copy.47, pred[]{:T(512)} %bitcast.4, f32[1,1,256,256]{2,1,3,0:T(1,128)S(1)} %collective-permute-done.31, ...), kind=kLoop, calls=%fused_computation.86 | loop fusion | flops 9961470 | bytes 4718602 | tf_op jit(solution)/shard_map/reduce_sum | solution.py:91
  380.4 18.7 %all-reduce.31 = (f32[1]{0:T(128)}, f32[1]{0:T(128)}) all-reduce(f32[1]{0:T(128)} %bitcast.20, f32[1]{0:T(128)} %bitcast.21), channel_id=1, replica_groups=mesh['gz'=8,'pair'=4] {'gz'}, use_global_device_ids=true, to_apply=%region_5.7 | all-reduce | flops 2 | bytes 16 | tf_op jit(solution)/shard_map/psum | solution.py:90
  399.0 1.4 multiply_dynamic-update-slice_fusion
  400.5 2.9 copy.44
  403.4 9.9 %all-reduce.30 = f32[4]{0:T(128)S(1)} all-reduce(f32[4]{0:T(128)S(1)} %multiply_dynamic-update-slice_fusion), channel_id=1, replica_groups=mesh['gz'=8,'pair'=4] {'pair'}, use_global_device_ids=true, to_apply=%add.30 | all-reduce | flops 4 | bytes 32
  (109 shorter events, 28.9 us)
Async XLA Ops:
  1.5 14.0 %collective-permute-start = (f32[1,1,256,256]{2,1,3,0:T(1,128)}, f32[1,1,256,256]{2,1,3,0:T(1,128)S(1)}, u32[]{:S(2)}, u32[]{:S(2)}) collective-permute-start(f32[1,1,256,256]{2,1,3,0:T(1,128)} %broadcast.199), channel_id=1, source_target_pairs={{4,0},{8,4},{12,8},{16,12},{20,16},{24,20},{28,24},{5,1},{9,5},{13... | collective-permute-start | bytes 786440 | tf_op jit(solution)/shard_map/ppermute | solution.py:20
  2.8 12.7 %collective-permute-start.1 = (f32[1,1,256,256]{2,1,3,0:T(1,128)}, f32[1,1,256,256]{2,1,3,0:T(1,128)}, u32[]{:S(2)}, u32[]{:S(2)}) collective-permute-start(f32[1,1,256,256]{2,1,3,0:T(1,128)} %broadcast.199), channel_id=1, source_target_pairs={{0,4},{4,8},{8,12},{12,16},{16,20},{20,24},{24,28},{1,5},{5,9},{9,... | collective-permute-start | bytes 786440 | tf_op jit(solution)/shard_map/ppermute | solution.py:17
  18.7 5.8 %collective-permute-start.2 = (f32[1,1,256,256]{2,1,3,0:T(1,128)S(1)}, f32[1,1,256,256]{2,1,3,0:T(1,128)S(1)}, u32[]{:S(2)}, u32[]{:S(2)}) collective-permute-start(f32[1,1,256,256]{2,1,3,0:T(1,128)S(1)} %get-tuple-element.45), channel_id=1, source_target_pairs={{4,0},{8,4},{12,8},{16,12},{20,16},{24,20},{28,24},{5,1},{9,5},{13... | collective-permute-start | bytes 786440 | tf_op jit(solution)/shard_map/ppermute | solution.py:20
  20.0 5.7 %collective-permute-start.3 = (f32[1,1,256,256]{2,1,3,0:T(1,128)S(1)}, f32[1,1,256,256]{2,1,3,0:T(1,128)S(1)}, u32[]{:S(2)}, u32[]{:S(2)}) collective-permute-start(f32[1,1,256,256]{2,1,3,0:T(1,128)S(1)} %get-tuple-element.46), channel_id=1, source_target_pairs={{0,4},{4,8},{8,12},{12,16},{16,20},{20,24},{24,28},{1,5},{5,9},{9,... | collective-permute-start | bytes 786440 | tf_op jit(solution)/shard_map/ppermute | solution.py:17
  28.0 14.4 %copy-start = (f32[1,8,256,256]{2,1,3,0:T(8,128)}, f32[1,8,256,256]{2,1,3,0:T(8,128)S(1)}, u32[]{:S(2)}) copy-start(f32[1,8,256,256]{2,1,3,0:T(8,128)S(1)} %fusion.14) | copy-start | bytes 6291460
  28.3 14.1 %collective-permute-start.4 = (f32[1,1,256,256]{2,1,3,0:T(1,128)S(1)}, f32[1,1,256,256]{2,1,3,0:T(1,128)S(1)}, u32[]{:S(2)}, u32[]{:S(2)}) collective-permute-start(f32[1,1,256,256]{2,1,3,0:T(1,128)S(1)} %get-tuple-element.43), channel_id=1, source_target_pairs={{4,0},{8,4},{12,8},{16,12},{20,16},{24,20},{28,24},{5,1},{9,5},{13... | collective-permute-start | bytes 786440 | tf_op jit(solution)/shard_map/ppermute | solution.py:20
  29.6 12.8 %collective-permute-start.5 = (f32[1,1,256,256]{2,1,3,0:T(1,128)S(1)}, f32[1,1,256,256]{2,1,3,0:T(1,128)S(1)}, u32[]{:S(2)}, u32[]{:S(2)}) collective-permute-start(f32[1,1,256,256]{2,1,3,0:T(1,128)S(1)} %get-tuple-element.44), channel_id=1, source_target_pairs={{0,4},{4,8},{8,12},{12,16},{16,20},{20,24},{24,28},{1,5},{5,9},{9,... | collective-permute-start | bytes 786440 | tf_op jit(solution)/shard_map/ppermute | solution.py:17
  36.1 189.2 %collective-permute-start.6 = (f32[1,1,128,128]{3,2,1,0:T(8,128)S(1)}, f32[1,1,128,128]{3,2,1,0:T(8,128)S(1)}, u32[]{:S(2)}, u32[]{:S(2)}) collective-permute-start(f32[1,1,128,128]{3,2,1,0:T(8,128)S(1)} %broadcast.203), channel_id=1, source_target_pairs={{4,0},{8,4},{12,8},{16,12},{20,16},{24,20},{28,24},{5,1},{9,5},{13... | collective-permute-start | bytes 196616 | tf_op jit(solution)/shard_map/ppermute | solution.py:20
  37.4 187.9 %collective-permute-start.7 = (f32[1,1,128,128]{3,2,1,0:T(8,128)S(1)}, f32[1,1,128,128]{3,2,1,0:T(8,128)S(1)}, u32[]{:S(2)}, u32[]{:S(2)}) collective-permute-start(f32[1,1,128,128]{3,2,1,0:T(8,128)S(1)} %broadcast.203), channel_id=1, source_target_pairs={{0,4},{4,8},{8,12},{12,16},{16,20},{20,24},{24,28},{1,5},{5,9},{9,... | collective-permute-start | bytes 196616 | tf_op jit(solution)/shard_map/ppermute | solution.py:17
  225.5 5.6 %collective-permute-start.8 = (f32[1,1,128,128]{3,2,1,0:T(8,128)S(1)}, f32[1,1,128,128]{3,2,1,0:T(8,128)S(1)}, u32[]{:S(2)}, u32[]{:S(2)}) collective-permute-start(f32[1,1,128,128]{3,2,1,0:T(8,128)S(1)} %get-tuple-element.53), channel_id=1, source_target_pairs={{4,0},{8,4},{12,8},{16,12},{20,16},{24,20},{28,24},{5,1},{9,5},{13... | collective-permute-start | bytes 196616 | tf_op jit(solution)/shard_map/ppermute | solution.py:20
  226.8 5.2 %collective-permute-start.9 = (f32[1,1,128,128]{3,2,1,0:T(8,128)S(1)}, f32[1,1,128,128]{3,2,1,0:T(8,128)S(1)}, u32[]{:S(2)}, u32[]{:S(2)}) collective-permute-start(f32[1,1,128,128]{3,2,1,0:T(8,128)S(1)} %get-tuple-element.54), channel_id=1, source_target_pairs={{0,4},{4,8},{8,12},{12,16},{16,20},{20,24},{24,28},{1,5},{5,9},{9,... | collective-permute-start | bytes 196616 | tf_op jit(solution)/shard_map/ppermute | solution.py:17
  232.2 12.3 %copy-start.2 = (f32[1,4,128,128]{3,2,1,0:T(8,128)}, f32[1,4,128,128]{3,2,1,0:T(8,128)S(1)}, u32[]{:S(2)}) copy-start(f32[1,4,128,128]{3,2,1,0:T(8,128)S(1)} %fusion.66) | copy-start | bytes 786436
  232.2 12.2 %collective-permute-start.10 = (f32[1,1,128,128]{3,2,1,0:T(8,128)S(1)}, f32[1,1,128,128]{3,2,1,0:T(8,128)S(1)}, u32[]{:S(2)}, u32[]{:S(2)}) collective-permute-start(f32[1,1,128,128]{3,2,1,0:T(8,128)S(1)} %get-tuple-element.51), channel_id=1, source_target_pairs={{4,0},{8,4},{12,8},{16,12},{20,16},{24,20},{28,24},{5,1},{9,5},{13... | collective-permute-start | bytes 196616 | tf_op jit(solution)/shard_map/ppermute | solution.py:20
  233.5 10.9 %collective-permute-start.11 = (f32[1,1,128,128]{3,2,1,0:T(8,128)S(1)}, f32[1,1,128,128]{3,2,1,0:T(8,128)S(1)}, u32[]{:S(2)}, u32[]{:S(2)}) collective-permute-start(f32[1,1,128,128]{3,2,1,0:T(8,128)S(1)} %get-tuple-element.52), channel_id=1, source_target_pairs={{0,4},{4,8},{8,12},{12,16},{16,20},{20,24},{24,28},{1,5},{5,9},{9,... | collective-permute-start | bytes 196616 | tf_op jit(solution)/shard_map/ppermute | solution.py:17
  238.2 31.5 %collective-permute-start.12 = (f32[1,1,64,64]{3,2,1,0:T(8,128)S(1)}, f32[1,1,64,64]{3,2,1,0:T(8,128)S(1)}, u32[]{:S(2)}, u32[]{:S(2)}) collective-permute-start(f32[1,1,64,64]{3,2,1,0:T(8,128)S(1)} %broadcast.208), channel_id=1, source_target_pairs={{4,0},{8,4},{12,8},{16,12},{20,16},{24,20},{28,24},{5,1},{9,5},{13... | collective-permute-start | bytes 49160 | tf_op jit(solution)/shard_map/ppermute | solution.py:20
  239.5 30.3 %collective-permute-start.13 = (f32[1,1,64,64]{3,2,1,0:T(8,128)S(1)}, f32[1,1,64,64]{3,2,1,0:T(8,128)S(1)}, u32[]{:S(2)}, u32[]{:S(2)}) collective-permute-start(f32[1,1,64,64]{3,2,1,0:T(8,128)S(1)} %broadcast.208), channel_id=1, source_target_pairs={{0,4},{4,8},{8,12},{12,16},{16,20},{20,24},{24,28},{1,5},{5,9},{9,... | collective-permute-start | bytes 49160 | tf_op jit(solution)/shard_map/ppermute | solution.py:17
  269.9 5.6 %collective-permute-start.14 = (f32[1,1,64,64]{3,2,1,0:T(8,128)S(1)}, f32[1,1,64,64]{3,2,1,0:T(8,128)S(1)}, u32[]{:S(2)}, u32[]{:S(2)}) collective-permute-start(f32[1,1,64,64]{3,2,1,0:T(8,128)S(1)} %get-tuple-element.63), channel_id=1, source_target_pairs={{4,0},{8,4},{12,8},{16,12},{20,16},{24,20},{28,24},{5,1},{9,5},{13... | collective-permute-start | bytes 49160 | tf_op jit(solution)/shard_map/ppermute | solution.py:20
  271.2 5.1 %collective-permute-start.15 = (f32[1,1,64,64]{3,2,1,0:T(8,128)S(1)}, f32[1,1,64,64]{3,2,1,0:T(8,128)S(1)}, u32[]{:S(2)}, u32[]{:S(2)}) collective-permute-start(f32[1,1,64,64]{3,2,1,0:T(8,128)S(1)} %get-tuple-element.64), channel_id=1, source_target_pairs={{0,4},{4,8},{8,12},{12,16},{16,20},{20,24},{24,28},{1,5},{5,9},{9,... | collective-permute-start | bytes 49160 | tf_op jit(solution)/shard_map/ppermute | solution.py:17
  276.5 5.9 %collective-permute-start.16 = (f32[1,1,64,64]{3,2,1,0:T(8,128)S(1)}, f32[1,1,64,64]{3,2,1,0:T(8,128)S(1)}, u32[]{:S(2)}, u32[]{:S(2)}) collective-permute-start(f32[1,1,64,64]{3,2,1,0:T(8,128)S(1)} %get-tuple-element.61), channel_id=1, source_target_pairs={{4,0},{8,4},{12,8},{16,12},{20,16},{24,20},{28,24},{5,1},{9,5},{13... | collective-permute-start | bytes 49160 | tf_op jit(solution)/shard_map/ppermute | solution.py:20
  277.8 5.3 %collective-permute-start.17 = (f32[1,1,64,64]{3,2,1,0:T(8,128)S(1)}, f32[1,1,64,64]{3,2,1,0:T(8,128)S(1)}, u32[]{:S(2)}, u32[]{:S(2)}) collective-permute-start(f32[1,1,64,64]{3,2,1,0:T(8,128)S(1)} %get-tuple-element.62), channel_id=1, source_target_pairs={{0,4},{4,8},{8,12},{12,16},{16,20},{20,24},{24,28},{1,5},{5,9},{9,... | collective-permute-start | bytes 49160 | tf_op jit(solution)/shard_map/ppermute | solution.py:17
  304.2 13.2 %copy-start.3 = (f32[1,4,128,128]{3,2,1,0:T(8,128)S(1)}, f32[1,4,128,128]{3,2,1,0:T(8,128)}, u32[]{:S(2)}) copy-start(f32[1,4,128,128]{3,2,1,0:T(8,128)} %copy-done.2) | copy-start | bytes 786436
  305.0 4.3 %collective-permute-start.18 = (f32[1,1,64,64]{3,2,1,0:T(8,128)S(1)}, f32[1,1,64,64]{3,2,1,0:T(8,128)S(1)}, u32[]{:S(2)}, u32[]{:S(2)}) collective-permute-start(f32[1,1,64,64]{3,2,1,0:T(8,128)S(1)} %get-tuple-element.59), channel_id=1, source_target_pairs={{4,0},{8,4},{12,8},{16,12},{20,16},{24,20},{28,24},{5,1},{9,5},{13... | collective-permute-start | bytes 49160 | tf_op jit(solution)/shard_map/ppermute | solution.py:20
  306.3 3.9 collective-permute-start.19
  310.4 5.6 %collective-permute-start.20 = (f32[1,1,64,64]{3,2,1,0:T(8,128)S(1)}, f32[1,1,64,64]{3,2,1,0:T(8,128)S(1)}, u32[]{:S(2)}, u32[]{:S(2)}) collective-permute-start(f32[1,1,64,64]{3,2,1,0:T(8,128)S(1)} %get-tuple-element.57), channel_id=1, source_target_pairs={{4,0},{8,4},{12,8},{16,12},{20,16},{24,20},{28,24},{5,1},{9,5},{13... | collective-permute-start | bytes 49160 | tf_op jit(solution)/shard_map/ppermute | solution.py:20
  311.7 5.1 %collective-permute-start.21 = (f32[1,1,64,64]{3,2,1,0:T(8,128)S(1)}, f32[1,1,64,64]{3,2,1,0:T(8,128)S(1)}, u32[]{:S(2)}, u32[]{:S(2)}) collective-permute-start(f32[1,1,64,64]{3,2,1,0:T(8,128)S(1)} %get-tuple-element.58), channel_id=1, source_target_pairs={{0,4},{4,8},{8,12},{12,16},{16,20},{20,24},{24,28},{1,5},{5,9},{9,... | collective-permute-start | bytes 49160 | tf_op jit(solution)/shard_map/ppermute | solution.py:17
  317.4 6.3 %collective-permute-start.22 = (f32[1,1,128,128]{3,2,1,0:T(8,128)S(1)}, f32[1,1,128,128]{3,2,1,0:T(8,128)S(1)}, u32[]{:S(2)}, u32[]{:S(2)}) collective-permute-start(f32[1,1,128,128]{3,2,1,0:T(8,128)S(1)} %get-tuple-element.49), channel_id=1, source_target_pairs={{4,0},{8,4},{12,8},{16,12},{20,16},{24,20},{28,24},{5,1},{9,5},{13... | collective-permute-start | bytes 196616 | tf_op jit(solution)/shard_map/ppermute | solution.py:20
  318.7 5.9 %collective-permute-start.23 = (f32[1,1,128,128]{3,2,1,0:T(8,128)S(1)}, f32[1,1,128,128]{3,2,1,0:T(8,128)S(1)}, u32[]{:S(2)}, u32[]{:S(2)}) collective-permute-start(f32[1,1,128,128]{3,2,1,0:T(8,128)S(1)} %get-tuple-element.50), channel_id=1, source_target_pairs={{0,4},{4,8},{8,12},{12,16},{16,20},{20,24},{24,28},{1,5},{5,9},{9,... | collective-permute-start | bytes 196616 | tf_op jit(solution)/shard_map/ppermute | solution.py:17
  324.9 6.6 %collective-permute-start.24 = (f32[1,1,128,128]{3,2,1,0:T(8,128)S(1)}, f32[1,1,128,128]{3,2,1,0:T(8,128)S(1)}, u32[]{:S(2)}, u32[]{:S(2)}) collective-permute-start(f32[1,1,128,128]{3,2,1,0:T(8,128)S(1)} %get-tuple-element.47), channel_id=1, source_target_pairs={{4,0},{8,4},{12,8},{16,12},{20,16},{24,20},{28,24},{5,1},{9,5},{13... | collective-permute-start | bytes 196616 | tf_op jit(solution)/shard_map/ppermute | solution.py:20
  326.2 6.2 %collective-permute-start.25 = (f32[1,1,128,128]{3,2,1,0:T(8,128)S(1)}, f32[1,1,128,128]{3,2,1,0:T(8,128)S(1)}, u32[]{:S(2)}, u32[]{:S(2)}) collective-permute-start(f32[1,1,128,128]{3,2,1,0:T(8,128)S(1)} %get-tuple-element.48), channel_id=1, source_target_pairs={{0,4},{4,8},{8,12},{12,16},{16,20},{20,24},{24,28},{1,5},{5,9},{9,... | collective-permute-start | bytes 196616 | tf_op jit(solution)/shard_map/ppermute | solution.py:17
  337.9 6.6 %collective-permute-start.26 = (f32[1,1,256,256]{2,1,3,0:T(1,128)S(1)}, f32[1,1,256,256]{2,1,3,0:T(1,128)S(1)}, u32[]{:S(2)}, u32[]{:S(2)}) collective-permute-start(f32[1,1,256,256]{2,1,3,0:T(1,128)S(1)} %get-tuple-element.41), channel_id=1, source_target_pairs={{4,0},{8,4},{12,8},{16,12},{20,16},{24,20},{28,24},{5,1},{9,5},{13... | collective-permute-start | bytes 786440 | tf_op jit(solution)/shard_map/ppermute | solution.py:20
  339.2 6.5 %collective-permute-start.27 = (f32[1,1,256,256]{2,1,3,0:T(1,128)S(1)}, f32[1,1,256,256]{2,1,3,0:T(1,128)S(1)}, u32[]{:S(2)}, u32[]{:S(2)}) collective-permute-start(f32[1,1,256,256]{2,1,3,0:T(1,128)S(1)} %get-tuple-element.42), channel_id=1, source_target_pairs={{0,4},{4,8},{8,12},{12,16},{16,20},{20,24},{24,28},{1,5},{5,9},{9,... | collective-permute-start | bytes 786440 | tf_op jit(solution)/shard_map/ppermute | solution.py:17
  348.2 8.4 %collective-permute-start.28 = (f32[1,1,256,256]{2,1,3,0:T(1,128)S(1)}, f32[1,1,256,256]{2,1,3,0:T(1,128)S(1)}, u32[]{:S(2)}, u32[]{:S(2)}) collective-permute-start(f32[1,1,256,256]{2,1,3,0:T(1,128)S(1)} %get-tuple-element.39), channel_id=1, source_target_pairs={{4,0},{8,4},{12,8},{16,12},{20,16},{24,20},{28,24},{5,1},{9,5},{13... | collective-permute-start | bytes 786440 | tf_op jit(solution)/shard_map/ppermute | solution.py:20
  349.5 21.2 %copy-start.4 = (u32[32]{0:T(128)S(1)}, u32[32]{0:T(128)}, u32[]{:S(2)}) copy-start(u32[32]{0:T(128)} %constant.162) | copy-start | bytes 388
  349.5 8.2 %collective-permute-start.29 = (f32[1,1,256,256]{2,1,3,0:T(1,128)S(1)}, f32[1,1,256,256]{2,1,3,0:T(1,128)S(1)}, u32[]{:S(2)}, u32[]{:S(2)}) collective-permute-start(f32[1,1,256,256]{2,1,3,0:T(1,128)S(1)} %get-tuple-element.40), channel_id=1, source_target_pairs={{0,4},{4,8},{8,12},{12,16},{16,20},{20,24},{24,28},{1,5},{5,9},{9,... | collective-permute-start | bytes 786440 | tf_op jit(solution)/shard_map/ppermute | solution.py:17
  359.9 1.4 copy-start.1
  361.5 9.8 %collective-permute-start.30 = (f32[1,1,256,256]{2,1,3,0:T(1,128)S(1)}, f32[1,1,256,256]{2,1,3,0:T(1,128)S(1)}, u32[]{:S(2)}, u32[]{:S(2)}) collective-permute-start(f32[1,1,256,256]{2,1,3,0:T(1,128)S(1)} %get-tuple-element.37), channel_id=1, source_target_pairs={{4,0},{8,4},{12,8},{16,12},{20,16},{24,20},{28,24},{5,1},{9,5},{13... | collective-permute-start | bytes 786440 | tf_op jit(solution)/shard_map/ppermute | solution.py:20
  362.8 8.5 %collective-permute-start.31 = (f32[1,1,256,256]{2,1,3,0:T(1,128)S(1)}, f32[1,1,256,256]{2,1,3,0:T(1,128)S(1)}, u32[]{:S(2)}, u32[]{:S(2)}) collective-permute-start(f32[1,1,256,256]{2,1,3,0:T(1,128)S(1)} %get-tuple-element.38), channel_id=1, source_target_pairs={{0,4},{4,8},{8,12},{12,16},{16,20},{20,24},{24,28},{1,5},{5,9},{9,... | collective-permute-start | bytes 786440 | tf_op jit(solution)/shard_map/ppermute | solution.py:17
